TPU v7x, 32 devices: a whole 2x2x4 slice. The times are simulated.
32 devices in a mesh: ctx: 8 (over y, x, core), tp: 4 (over z).
Axes of the slice: x: 2, y: 2, z: 4, core: 2. Of those that a mesh axis runs over, the one named last changes fastest.
Arguments:
- activations: bfloat16 [2048, 4096], P(('ctx', 'tp')), may hold values from -6 to 6
- input_proj: bfloat16 [4096, 3, 2048], P(None, None, 'tp'), may hold values from -0.09375 to 0.09375
- short_taps: float32 [3, 7, 2048], P(None, None, 'tp'), may hold values from -2 to 2
- medium_taps: float32 [128, 128], P('tp'), may hold values from -0.5 to 0.5
- skip_gain: float32 [2048], P('tp'), may hold values from -4 to 4
- output_proj: bfloat16 [2048, 4096], P('tp'), may hold values from -0.125 to 0.125
- out_grad: bfloat16 [2048, 4096], P(('ctx', 'tp')), may hold values from -6 to 6
Outputs:
- layer_out: bfloat16 [2048, 4096], P(('ctx', 'tp'))
- act_grad: bfloat16 [2048, 4096], P(('ctx', 'tp'))
All inputs are finite; a program needn't handle non-finite values.
Results may differ from a plain program's by a relative error of at most 0.015.
Values may be sent and summed in bfloat16 or wider, within the bound.
A program may use at most 128 MiB of HBM per device.

v0:
```python
import jax
import jax.numpy as jnp
from jax import lax
from jax.sharding import PartitionSpec as P

GROUP_SIZE = 16


def from_behind(x, axis, by):
    devices = lax.axis_size(axis)
    pairs = [(i, i + by) for i in range(devices) if 0 <= i + by < devices]
    return lax.ppermute(x, axis, pairs)


def banded(head, row_count, col_count):
    groups, taps = head.shape
    period = col_count + 1
    padded = jnp.concatenate([head, jnp.zeros((groups, period - taps), jnp.float32)], axis=1)
    tiled = jnp.tile(padded, (1, row_count))[:, : row_count * col_count]
    return tiled.reshape(groups, row_count, col_count)


def grouped_conv(head, source, row_count, group_size):
    span = head.shape[1]
    length, channels = source.shape
    tiles = -(-row_count // span)
    needed = (tiles + 1) * span
    kept = source
    kept = jnp.concatenate(
        [kept, jnp.zeros((needed - kept.shape[0], channels), jnp.float32)], axis=0
    )
    shaped = kept.reshape(tiles + 1, span, channels // group_size, group_size)
    window = jnp.concatenate([shaped[:-1], shaped[1:]], axis=1)
    band = banded(head, span, 2 * span)
    result = jnp.einsum("gtk,bkgc->btgc", band, window, precision=lax.Precision.HIGHEST)
    return result.reshape(tiles * span, channels)[:row_count]


def short_sum(source, taps, length, causal):
    total = jnp.zeros((length,) + source.shape[1:], jnp.float32)
    count = taps.shape[1]
    for lag in range(count):
        offset = count - 1 - lag if causal else lag
        total = total + taps[:, lag, :] * source[offset : offset + length].astype(jnp.float32)
    return total


def body(activations, input_proj, short_taps, medium_taps, skip_gain, output_proj, out_grad):
    tok_dev, width = activations.shape
    channels = input_proj.shape[2]
    med_span = medium_taps.shape[1]
    short_span = short_taps.shape[1]
    halo_rows = med_span + short_span - 2
    lead = short_span - 1
    flat_proj = input_proj.reshape(width, 3 * channels)
    contract = (((1,), (1,)), ((), ()))
    full_rows, full_grad = (
        lax.all_gather(activations, "tp", axis=0, tiled=True),
        lax.all_gather(out_grad, "tp", axis=0, tiled=True),
    )
    projected = jnp.dot(full_rows, flat_proj, preferred_element_type=jnp.float32).astype(
        jnp.bfloat16
    )
    block_rows = projected.shape[0]
    before = from_behind(projected[block_rows - halo_rows :], "ctx", 1)
    extended = jnp.concatenate([before, projected], axis=0).reshape(
        block_rows + halo_rows, 3, channels
    )
    conv_rows = block_rows + med_span - 1
    filtered = short_sum(extended, short_taps, conv_rows, True).astype(jnp.bfloat16)
    query = filtered[med_span - 1 :, 0].astype(jnp.float32)
    keyed = filtered[:, 1]
    valued = filtered[:, 2]
    mixed = keyed.astype(jnp.float32) * valued.astype(jnp.float32)
    inner = (
        grouped_conv(medium_taps[:, ::-1], mixed, block_rows, GROUP_SIZE)
        + skip_gain * mixed[med_span - 1 :]
    )
    gated = (query * inner).astype(jnp.bfloat16)
    part = gated
    layer_out = lax.psum_scatter(
        jnp.dot(part, output_proj, preferred_element_type=jnp.float32).astype(jnp.bfloat16),
        "tp",
        scatter_dimension=0,
        tiled=True,
    )
    grad_gated = lax.dot_general(
        full_grad, output_proj, contract, preferred_element_type=jnp.float32
    )
    grad_query = (grad_gated * inner).astype(jnp.bfloat16)
    grad_inner = (grad_gated * query).astype(jnp.bfloat16)
    own_key = keyed[med_span - 1 :]
    own_value = valued[med_span - 1 :]
    head = jnp.concatenate(
        [grad_inner[:halo_rows], grad_query[:lead], own_key[:lead], own_value[:lead]], axis=0
    )
    after = from_behind(head, "ctx", -1)
    inner_ext = jnp.concatenate([grad_inner, after[:halo_rows]], axis=0).astype(jnp.float32)
    query_ext = jnp.concatenate([grad_query, after[halo_rows : halo_rows + lead]], axis=0).astype(
        jnp.float32
    )
    key_ext = jnp.concatenate(
        [own_key, after[halo_rows + lead : halo_rows + 2 * lead]], axis=0
    ).astype(jnp.float32)
    value_ext = jnp.concatenate([own_value, after[halo_rows + 2 * lead :]], axis=0).astype(
        jnp.float32
    )
    grad_count = block_rows + lead
    grad_mixed = (
        grouped_conv(medium_taps, inner_ext, grad_count, GROUP_SIZE)
        + skip_gain * inner_ext[:grad_count]
    )
    grad_filtered = jnp.stack([query_ext, grad_mixed * value_ext, grad_mixed * key_ext], axis=1)
    grad_projected = short_sum(grad_filtered, short_taps, block_rows, False).astype(jnp.bfloat16)
    grad_projected = grad_projected.reshape(block_rows, 3 * channels)
    part = grad_projected
    act_grad = lax.psum_scatter(
        lax.dot_general(part, flat_proj, contract, preferred_element_type=jnp.float32).astype(
            jnp.bfloat16
        ),
        "tp",
        scatter_dimension=0,
        tiled=True,
    )
    return (layer_out, act_grad)


def solution(mesh):
    placed = (
        P(("ctx", "tp"), None),
        P(None, None, "tp"),
        P(None, None, "tp"),
        P("tp", None),
        P("tp"),
        P("tp", None),
        P(("ctx", "tp"), None),
    )
    return jax.shard_map(
        body,
        mesh=mesh,
        in_specs=placed,
        out_specs=(P(("ctx", "tp"), None), P(("ctx", "tp"), None)),
        check_vma=False,
    )
```

profile of v0, /device:TPU:0, one launch (start us, length us, event | category | flops | bytes accessed | tf_op | source)
XLA Modules:
  0.0 243.7 jit_solution(3685538261319816156)
XLA Ops:
  7.2 0.7 all-gather.3.cloned.1.call-update
  7.9 0.7 all-gather.5.cloned.1.call-update
  8.7 17.0 %copy.19 = bf16[4096,3,512]{0,2,1:T(8,128)(2,1)} copy(bf16[4096,3,512]{2,0,1:T(8,128)(2,1)} %param.8) | data formatting | bytes 25165824 | tf_op args[1]
  25.8 0.6 copy.71
  26.4 3.1 %tile.8 = f32[32,128,257]{2,1,0:T(8,128)} broadcast(f32[32,257]{1,0:T(8,128)S(1)} %concatenate.50), dimensions={0,2} | broadcast | bytes 4243584 | tf_op jit(solution)/shard_map/tile | solution.py:19
  29.5 6.7 %tile.9 = f32[32,32896]{1,0:T(8,128)} reshape(f32[32,128,257]{2,1,0:T(8,128)} %tile.8) | data formatting | bytes 8421376 | tf_op jit(solution)/shard_map/tile | solution.py:19
  36.2 2.2 slice-done
  38.4 3.3 %copy.56 = f32[4,8,128,256]{3,2,1,0:T(8,128)} copy(f32[4,8,128,256]{3,1,2,0:T(8,128)S(1)} %bitcast.114) | data formatting | bytes 8388608
  41.8 0.6 copy_bitcast_fusion.2
  42.4 15.6 %all-gather.3.cloned.1.call-done = bf16[256,4096]{1,0:T(8,128)(2,1)} async-done(((bf16[64,4096]{1,0:T(8,128)(2,1)}), bf16[256,4096]{1,0:T(8,128)(2,1)}) %all-gather.3.cloned.1.call-update) | async-done | bytes 2097168 | tf_op jit(solution)/shard_map/all_gather | solution.py:58
  58.0 8.7 %convolution_convert_fusion.1 = bf16[256,1536]{1,0:T(8,128)(2,1)S(1)} fusion(bf16[256,4096]{1,0:T(8,128)(2,1)} %all-gather.3.cloned.1.call-done, bf16[4096,1536]{0,1:T(8,128)(2,1)} %bitcast.118), kind=kOutput, calls=%fused_computation.7 | convolution fusion | flops 3221618688 | bytes 15466496 | tf_op jit(solution)/shard_map/dot_general | solution.py:61
  66.7 1.8 collective-permute-start
  68.5 0.6 copy_bitcast_fusion.4
  69.1 0.6 copy_bitcast_fusion.6
  69.7 6.0 %fusion.26 = (f32[383,1536]{1,0:T(8,128)}, f32[383,1536]{1,0:T(8,128)}, f32[383,1536]{1,0:T(8,128)}, f32[383,1536]{1,0:T(8,128)}, f32[383,1536]{1,0:T(8,128)}, /*index=5*/f32[383,1536]{1,0:T(8,128)}, f32[383,1536]{1,0:T(8,128)}) fusion(bf16[256,1536]{1,0:T(8,128)(2,1)S(1)} %convolution_convert_fusion.1, bf16[133,1536]{1,0:T(8,128)(2,1)S(1)} %collective-permute-done), kind=kLoop, calls=%fused_computation.44 | loop fusion | flops 16472064 | bytes 17667072 | tf_op jit(solution)/shard_map/convert_element_type | solution.py:44
  75.7 3.1 %copy.32 = f32[383,1536]{0,1:T(8,128)} copy(f32[383,1536]{1,0:T(8,128)} %get-tuple-element.9) | data formatting | bytes 4706304 | tf_op jit(solution)/shard_map/convert_element_type | solution.py:44
  78.8 2.0 copy.33
  80.9 3.1 %copy.30 = f32[383,1536]{0,1:T(8,128)} copy(f32[383,1536]{1,0:T(8,128)} %get-tuple-element.10) | data formatting | bytes 4706304 | tf_op jit(solution)/shard_map/convert_element_type | solution.py:44
  84.0 3.1 %copy.31 = f32[383,3,512]{2,0,1:T(8,128)} copy(f32[383,3,512]{0,2,1:T(8,128)} %bitcast.120) | data formatting | bytes 4706304 | tf_op jit(solution)/shard_map/convert_element_type | solution.py:44
  87.1 3.1 %copy.28 = f32[383,1536]{0,1:T(8,128)} copy(f32[383,1536]{1,0:T(8,128)} %get-tuple-element.8) | data formatting | bytes 4706304 | tf_op jit(solution)/shard_map/convert_element_type | solution.py:44
  90.2 3.2 %copy.29 = f32[383,3,512]{2,0,1:T(8,128)} copy(f32[383,3,512]{0,2,1:T(8,128)} %bitcast.121) | data formatting | bytes 4706304 | tf_op jit(solution)/shard_map/convert_element_type | solution.py:44
  93.4 3.1 %copy.26 = f32[383,1536]{0,1:T(8,128)} copy(f32[383,1536]{1,0:T(8,128)} %get-tuple-element.7) | data formatting | bytes 4706304 | tf_op jit(solution)/shard_map/convert_element_type | solution.py:44
  96.5 3.1 %copy.27 = f32[383,3,512]{2,0,1:T(8,128)} copy(f32[383,3,512]{0,2,1:T(8,128)} %bitcast.122) | data formatting | bytes 4706304 | tf_op jit(solution)/shard_map/convert_element_type | solution.py:44
  99.5 3.1 %copy.24 = f32[383,1536]{0,1:T(8,128)} copy(f32[383,1536]{1,0:T(8,128)} %get-tuple-element.6) | data formatting | bytes 4706304 | tf_op jit(solution)/shard_map/convert_element_type | solution.py:44
  102.6 3.1 %copy.25 = f32[383,3,512]{2,0,1:T(8,128)} copy(f32[383,3,512]{0,2,1:T(8,128)} %bitcast.123) | data formatting | bytes 4706304 | tf_op jit(solution)/shard_map/convert_element_type | solution.py:44
  105.7 3.1 %copy.22 = f32[383,1536]{0,1:T(8,128)} copy(f32[383,1536]{1,0:T(8,128)} %get-tuple-element.5) | data formatting | bytes 4706304 | tf_op jit(solution)/shard_map/convert_element_type | solution.py:44
  108.8 3.1 %copy.23 = f32[383,3,512]{2,0,1:T(8,128)} copy(f32[383,3,512]{0,2,1:T(8,128)} %bitcast.124) | data formatting | bytes 4706304 | tf_op jit(solution)/shard_map/convert_element_type | solution.py:44
  111.9 3.1 %copy.20 = f32[383,1536]{0,1:T(8,128)} copy(f32[383,1536]{1,0:T(8,128)} %get-tuple-element.4) | data formatting | bytes 4706304 | tf_op jit(solution)/shard_map/convert_element_type | solution.py:44
  115.0 3.1 %copy.21 = f32[383,3,512]{2,0,1:T(8,128)} copy(f32[383,3,512]{0,2,1:T(8,128)} %bitcast.125) | data formatting | bytes 4706304 | tf_op jit(solution)/shard_map/convert_element_type | solution.py:44
  118.1 7.3 %add_convert_fusion = bf16[383,3,512]{2,0,1:T(8,128)(2,1)S(1)} fusion(f32[383,3,512]{2,0,1:T(8,128)S(1)} %copy.33, f32[383,3,512]{2,0,1:T(8,128)} %copy.31, f32[383,3,512]{2,0,1:T(8,128)} %copy.29, f32[383,3,512]{2,0,1:T(8,128)} %copy.27, f32[383,3,512]{2,0,1:T(8,128)} %copy.25, f32[383,3,512]{2,0,1:T(8,128)} %copy.23, f32[383,3,512]{2,0,1:T(8,128)} %copy.21, ...), kind=kLoop, calls=%fused_computation.14 | loop fusion | flops 8236032 | bytes 17691648 | tf_op jit(solution)/shard_map/convert_element_type | solution.py:70
  125.5 0.2 convert_multiply_fusion
  125.7 0.2 copy.35
  125.9 0.3 slice.201
  126.3 0.2 copy.34
  126.5 0.3 slice.199
  126.8 5.9 %fusion.20 = f32[2,128,32,16]{1,3,0,2:T(8,128)S(1)} fusion(f32[32,128,256,1]{2,1,0,3:T(8,128)} %bitcast.116, f32[2,128,32,16]{1,3,0,2:T(8,128)S(1)} %copy.37, f32[2,128,32,16]{1,3,0,2:T(8,128)S(1)} %copy.36), kind=kOutput, calls=%fused_computation.40 | convolution fusion | flops 402915328 | bytes 5767168 | tf_op jit(solution)/shard_map/gtk,bkgc->btgc/dot_general | solution.py:35
  132.7 0.3 copy.38
  133.1 0.2 copy.39
  133.3 4.8 %convolution_convert_fusion = bf16[256,4096]{1,0:T(8,128)(2,1)} fusion(bf16[512,4096]{1,0:T(8,128)(2,1)} %param.12, bf16[383,3,512]{2,0,1:T(8,128)(2,1)S(1)} %add_convert_fusion, f32[256,512]{1,0:T(8,128)S(1)} %copy.39, f32[383,1,512]{2,0,1:T(8,128)S(1)} %get-tuple-element.15, f32[512]{0:T(512)} %param.11), kind=kOutput, calls=%fused_computation.2 | convolution fusion | flops 1075445760 | bytes 7604224 | tf_op jit(solution)/shard_map/dot_general | solution.py:82
  138.1 0.3 reduce-scatter.5.cloned.1.call-start
  138.4 3.1 %tile.20 = f32[32,128,257]{2,1,0:T(8,128)} broadcast(f32[32,257]{1,0:T(8,128)S(1)} %concatenate.58), dimensions={0,2} | broadcast | bytes 4243584 | tf_op jit(solution)/shard_map/tile | solution.py:19
  141.5 6.6 %tile.21 = f32[32,32896]{1,0:T(8,128)} reshape(f32[32,128,257]{2,1,0:T(8,128)} %tile.20) | data formatting | bytes 8421376 | tf_op jit(solution)/shard_map/tile | solution.py:19
  148.1 2.6 %slice-done.1 = f32[32,32768]{1,0:T(8,128)S(1)} async-done(((f32[32,32896]{1,0:T(8,128)}), f32[32,32768]{1,0:T(8,128)S(1)}, s32[]{:S(2)}) %slice-start.1) | async-done | bytes 4194328 | tf_op jit(solution)/shard_map/slice | solution.py:19
  150.7 3.3 %copy.58 = f32[4,8,128,256]{3,2,1,0:T(8,128)} copy(f32[4,8,128,256]{3,1,2,0:T(8,128)S(1)} %bitcast.115) | data formatting | bytes 8388608
  154.0 4.2 %fusion.49 = (bf16[256,512]{1,0:T(8,128)(2,1)S(1)}, bf16[256,512]{1,0:T(8,128)(2,1)S(1)}) fusion(bf16[383,3,512]{2,0,1:T(8,128)(2,1)S(1)} %add_convert_fusion, f32[256,512]{1,0:T(8,128)S(1)} %copy.39, f32[383,1,512]{2,0,1:T(8,128)S(1)} %get-tuple-element.15, f32[512]{0:T(512)S(1)} %copy-done.14, bf16[256,4096]{1,0:T(8,128)(2,1)} %all-gather.5.cloned.1.call-done, ...), kind=kOutput, calls=%fused_computation.76 | convolution fusion | flops 1074659328 | bytes 8128512 | tf_op jit(solution)/shard_map/dot_general | solution.py:87
  158.2 0.7 copy-done.2
  159.0 1.3 collective-permute-start.1
  160.3 0.9 slice_bitcast_fusion.2
  161.2 5.8 %collective-permute-done.1 = bf16[151,512]{1,0:T(8,128)(2,1)S(1)} collective-permute-done((bf16[151,512]{1,0:T(8,128)(2,1)S(1)}, bf16[151,512]{1,0:T(8,128)(2,1)S(1)}, u32[]{:S(2)}, u32[]{:S(2)}) %collective-permute-start.1) | collective-permute-done | bytes 154656 | tf_op jit(solution)/shard_map/ppermute | solution.py:12
  167.0 0.6 copy-done.4
  167.8 1.1 fusion.57
  168.8 0.3 copy.41
  169.1 0.3 slice.216
  169.5 1.4 copy.40
  170.9 0.3 slice.214
  171.3 6.0 %fusion.15 = f32[3,128,32,16]{1,3,0,2:T(8,128)S(1)} fusion(f32[32,128,256,1]{2,1,0,3:T(8,128)} %bitcast.117, f32[3,128,32,16]{1,3,0,2:T(8,128)S(1)} %copy.43, f32[3,128,32,16]{1,3,0,2:T(8,128)S(1)} %copy.42), kind=kOutput, calls=%fused_computation.39 | convolution fusion | flops 604372992 | bytes 6553600 | tf_op jit(solution)/shard_map/gtk,bkgc->btgc/dot_general | solution.py:35
  177.4 0.4 copy.44
  177.9 0.2 copy.55
  178.1 0.8 slice_bitcast_fusion.5
  179.1 0.2 multiply_bitcast_fusion.1
  179.3 0.1 pad_maximum_fusion
  179.4 0.3 copy-done.7
  179.8 10.3 %fusion = bf16[256,4096]{1,0:T(8,128)(2,1)} fusion(bf16[4096,3,512]{2,0,1:T(8,128)(2,1)} %param.8, f32[262,3,512]{2,0,1:T(8,128)S(1)} %pad_maximum_fusion, f32[3,512]{1,0:T(4,128)S(1)} %copy-done.7, f32[3,512]{1,0:T(4,128)S(1)} %copy-done.8, f32[3,512]{1,0:T(4,128)S(1)} %copy-done.9, f32[3,512]{1,0:T(4,128)S(1)} %copy-done.10, f32[3,512]{1,0:T(4,128)S(1)} %copy-done.11, ...), kind=kOutput, calls=%fused_computation.1 | convolution fusion | flops 3227779072 | bytes 25747456 | tf_op jit(solution)/shard_map/dot_general | solution.py:118
  190.2 47.0 %reduce-scatter.5.cloned.1.call-done = bf16[64,4096]{1,0:T(8,128)(2,1)} async-done(((bf16[256,4096]{1,0:T(8,128)(2,1)}), bf16[64,4096]{1,0:T(8,128)(2,1)}) %reduce-scatter.5.cloned.1.call-update) | async-done | bytes 524304 | tf_op jit(solution)/shard_map/reduce_scatter | solution.py:117
  (57 shorter events, 1.1 us)
Async XLA Ops:
  7.2 50.8 %all-gather.3.cloned.1.call-start = ((), (), s32[]{:S(2)}) async-start(), calls=%async_computation.2 | async-start | bytes 2621440 | tf_op jit(solution)/shard_map/all_gather | solution.py:58
  7.9 146.1 %all-gather.5.cloned.1.call-start = ((), (), s32[]{:S(2)}) async-start(), calls=%async_computation.4 | async-start | bytes 2621440 | tf_op jit(solution)/shard_map/all_gather | solution.py:59
  8.6 17.1 %copy-start.6 = (f32[3,7,512]{2,1,0:T(8,128)S(1)}, f32[3,7,512]{2,1,0:T(8,128)}, u32[]{:S(2)}) copy-start(f32[3,7,512]{2,1,0:T(8,128)} %param.9) | copy-start | bytes 129028
  8.7 17.7 %copy-start.5 = (f32[32,128]{1,0:T(8,128)S(1)}, f32[32,128]{1,0:T(8,128)}, u32[]{:S(2)}) copy-start(f32[32,128]{1,0:T(8,128)} %param.10) | copy-start | bytes 49156
  8.7 181.5 %reduce-scatter.3.cloned.1.call-start = ((), (), s32[]{:S(2)}) async-start(), calls=%async_computation.3 | async-start | bytes 2621440 | tf_op jit(solution)/shard_map/reduce_scatter | solution.py:81
  36.2 2.2 slice-start
  66.7 3.0 %collective-permute-start = (bf16[133,1536]{1,0:T(8,128)(2,1)S(1)}, bf16[133,1536]{1,0:T(8,128)(2,1)S(1)}, u32[]{:S(2)}, u32[]{:S(2)}) collective-permute-start(bf16[133,1536]{1,0:T(8,128)(2,1)S(1)} %slice.233), channel_id=1, source_target_pairs={{0,4},{4,8},{8,12},{12,16},{16,20},{20,24},{24,28},{1,5},{5,9},{9,... | collective-permute-start | bytes 1225736 | tf_op jit(solution)/shard_map/ppermute | solution.py:12
  138.1 99.0 %reduce-scatter.5.cloned.1.call-start = ((), (), s32[]{:S(2)}) async-start(), calls=%async_computation.5 | async-start | bytes 2621440 | tf_op jit(solution)/shard_map/reduce_scatter | solution.py:117
  148.1 2.6 %slice-start.1 = ((f32[32,32896]{1,0:T(8,128)}), f32[32,32768]{1,0:T(8,128)S(1)}, s32[]{:S(2)}) async-start(f32[32,32896]{1,0:T(8,128)} %tile.21), calls=%async_computation.7 | async-start | bytes 8388608 | tf_op jit(solution)/shard_map/slice | solution.py:19
  150.7 3.3 %copy-start.14 = (f32[512]{0:T(512)S(1)}, f32[512]{0:T(512)}, u32[]{:S(2)}) copy-start(f32[512]{0:T(512)} %param.11) | copy-start | bytes 6148
  158.2 0.7 copy-start.2
  159.0 8.0 %collective-permute-start.1 = (bf16[151,512]{1,0:T(8,128)(2,1)S(1)}, bf16[151,512]{1,0:T(8,128)(2,1)S(1)}, u32[]{:S(2)}, u32[]{:S(2)}) collective-permute-start(bf16[151,512]{1,0:T(8,128)(2,1)S(1)} %pad_maximum_fusion.2), channel_id=1, source_target_pairs={{4,0},{8,4},{12,8},{16,12},{20,16},{24,20},{28,24},{5,1},{9,5},{13... | collective-permute-start | bytes 463880 | tf_op jit(solution)/shard_map/ppermute | solution.py:12
  167.0 0.7 copy-start.4
  177.3 1.6 copy-start.3
  177.8 1.2 copy-start
  177.8 1.2 copy-start.1
  179.0 0.7 copy-start.7
  179.0 0.7 copy-start.8
  179.0 0.7 copy-start.9
  179.0 0.7 copy-start.10
  179.1 0.7 copy-start.11
  179.1 0.7 copy-start.12
  179.1 0.7 copy-start.13
Sparse Core Ops, SparseCore 0:
  9.5 48.3 all-gather.2
  59.5 44.4 all-gather.4
  138.2 48.7 reduce-scatter.2
  190.3 46.8 reduce-scatter.4
where the time goes:
time: 245 us; the launch traced here: 244 us
  local copies, waits for them, and re-layouts  102 us (42%)
  waiting for transfers between devices  69.9 us (29%)
  matrix products  39.9 us (16%)
  between operations  14.2 us (6%)
  other arithmetic  14 us (6%)
  starting transfers between devices  3.45 us (1%)
    reduce_scatter x1, waiting for transfers between devices, body(): lax.psum_scatter(lax.dot_general(part, flat_proj, contract, preferred_ele...  47 us
    convert_element_type x14, local copies, waits for them, and re-layouts, short_sum(): source[offset:offset + length].astype(jnp.float32)  42.4 us
    unnamed x40, local copies, waits for them, and re-layouts  28.1 us
    another operation x4, local copies, waits for them, and re-layouts, banded(): tiled = jnp.tile(padded, (1, row_count))[:, :row_count * col_count]  19.5 us
    all_gather x1, waiting for transfers between devices, body(): lax.all_gather(activations, 'tp', axis=0, tiled=True)  15.6 us
    dot_general x2, matrix products, grouped_conv(): jnp.einsum('gtk,bkgc->btgc', band, window, precision=lax.Precision.HIGHEST)  11.9 us
    dot_general x1, matrix products, body(): lax.dot_general(part, flat_proj, contract, preferred_element_type=jnp.flo...  10.3 us
    dot_general x1, matrix products, body(): jnp.dot(full_rows, flat_proj, preferred_element_type=jnp.float32)  8.65 us
  transfers between devices with their start and end apart: 6, of which 3 were waited for; matrix products, arithmetic and copies ran while one was open for 61% of the time, Pallas kernels for 0%

commit v1 on v0

v1 whole, which is shorter than its diff:
```python
import functools

import jax
import jax.numpy as jnp
from jax import lax
from jax.experimental import pallas as pl
from jax.experimental.pallas import tpu as pltpu
from jax.sharding import PartitionSpec as P

GROUP_SIZE = 16
LANES = 128
MESH = pl.DeviceIdType.MESH
F32 = jnp.float32
BF16 = jnp.bfloat16
NT = (((1,), (1,)), ((), ()))


def kernel(
    n, blocks, halo, lead,
    act_hbm, w_hbm, short_ref, med_ref, skip_ref, o_hbm, grad_hbm,
    out_ref, dact_ref,
    w, o, acts, grads, taps, pext, bext, gext, query, inner, gated, ggate, gproj, shifted,
    rs1, rs1_l, rs1_r, rs2, rs2_l, rs2_r,
    local_sem, bar_send, halo_send, halo_recv, *sems,
):
    me = lax.axis_index("tp")
    blk = lax.axis_index("ctx")
    rows, width = act_hbm.shape
    channels = w_hbm.shape[2]
    total = rows * n
    span = med_ref.shape[1]
    shorts = short_ref.shape[1]
    tiles = channels // LANES
    right = {"ctx": blk, "tp": me + 1}
    left = {"ctx": blk, "tp": me - 1}
    has_right = me + 1 < n
    has_left = me > 0
    has_next = blk + 1 < blocks
    has_prev = blk > 0

    def to(src, dst, send, recv, where):
        return pltpu.make_async_remote_copy(
            src_ref=src, dst_ref=dst, send_sem=send, recv_sem=recv,
            device_id=where, device_id_type=MESH,
        )

    loads = [
        pltpu.make_async_copy(act_hbm, acts.at[me], local_sem.at[0]),
        pltpu.make_async_copy(w_hbm, w, local_sem.at[1]),
        pltpu.make_async_copy(grad_hbm, grads.at[me], local_sem.at[2]),
        pltpu.make_async_copy(o_hbm, o, local_sem.at[3]),
    ]
    for load in loads:
        load.start()

    barrier = pltpu.get_barrier_semaphore()
    nbr = [
        (has_right, right), (has_left, left),
        (has_next, {"ctx": blk + 1, "tp": me}), (has_prev, {"ctx": blk - 1, "tp": me}),
    ]
    for cond, where in nbr:
        @pl.when(cond)
        def _(where=where):
            pl.semaphore_signal(barrier, inc=1, device_id=where, device_id_type=MESH)
    peers = sum(jnp.where(cond, 1, 0) for cond, _ in nbr)
    pl.semaphore_wait(barrier, peers)

    ga = sems[0:4]
    gg = sems[4:8]

    def send_right(buf, own, s, shard, first):
        src = own if first else buf.at[shard]
        to(src, buf.at[shard], s[0].at[shard], s[1].at[shard], right).start()

    def send_left(buf, own, s, shard, first):
        src = own if first else buf.at[shard]
        to(src, buf.at[shard], s[2].at[shard], s[3].at[shard], left).start()

    def from_left(buf, s, shard):
        to(buf.at[shard], buf.at[shard], s[0].at[shard], s[1].at[shard], left).wait_recv()

    def from_right(buf, s, shard):
        to(buf.at[shard], buf.at[shard], s[2].at[shard], s[3].at[shard], right).wait_recv()

    def gather_drain(buf, s):
        def one(i, carry):
            @pl.when(has_right & (i <= me))
            def _():
                to(buf.at[i], buf.at[i], s[0].at[i], s[1].at[i], right).wait_send()

            @pl.when(has_left & (i >= me))
            def _():
                to(buf.at[i], buf.at[i], s[2].at[i], s[3].at[i], left).wait_send()

            return carry

        lax.fori_loop(0, n, one, 0)

    def grad_own(step):
        @pl.when(has_right & (me == step))
        def _():
            send_right(grads, grad_hbm, gg, me, True)

        @pl.when(has_left & (n - 1 - me == step))
        def _():
            send_left(grads, grad_hbm, gg, me, True)

    @pl.when(has_right)
    def _():
        send_right(acts, act_hbm, ga, me, True)

    @pl.when(has_left)
    def _():
        send_left(acts, act_hbm, ga, me, True)

    grad_own(0)

    groups = med_ref.shape[0]
    ig = lax.broadcasted_iota(jnp.int32, (groups, channels), 0) * GROUP_SIZE
    ic = lax.broadcasted_iota(jnp.int32, (groups, channels), 1)
    spread = jnp.where((ic >= ig) & (ic < ig + GROUP_SIZE), 1.0, 0.0).astype(F32)
    taps[...] = lax.dot_general(
        med_ref[...], spread, (((0,), (0,)), ((), ())),
        precision=lax.Precision.HIGHEST, preferred_element_type=F32,
    )
    taps[0:1, :] = taps[0:1, :] + skip_ref[...]

    def project(shard):
        x = acts[shard]
        at = pl.ds(pl.multiple_of(halo + shard * rows, 16), rows)
        for s in range(3):
            pext[s, at, :] = jnp.dot(x, w[s], preferred_element_type=F32).astype(BF16)

    def grad_gate(shard):
        at = pl.ds(pl.multiple_of(shard * rows, 16), rows)
        ggate[at, :] = lax.dot_general(grads[shard], o[...], NT, preferred_element_type=F32)

    def step(buf, s, k, use):
        l, r = me - k, me + k

        @pl.when(l >= 0)
        def _():
            from_left(buf, s, l)

            @pl.when(has_right)
            def _():
                send_right(buf, None, s, l, False)

        @pl.when(r < n)
        def _():
            from_right(buf, s, r)

            @pl.when(has_left)
            def _():
                send_left(buf, None, s, r, False)

        if use is project:
            grad_own(k)

        @pl.when(l >= 0)
        def _():
            use(l)

        @pl.when(r < n)
        def _():
            use(r)

    loads[0].wait()
    loads[1].wait()
    project(me)

    def act_step(k, carry):
        step(acts, ga, k, project)
        return carry

    lax.fori_loop(1, n, act_step, 0)

    def fwd_halo():
        return to(
            pext.at[:, pl.ds(total, halo), :], pext.at[:, pl.ds(0, halo), :],
            halo_send.at[0], halo_recv.at[0], {"ctx": blk + 1, "tp": me},
        )

    def fwd_halo_in():
        return to(
            pext.at[:, pl.ds(total, halo), :], pext.at[:, pl.ds(0, halo), :],
            halo_send.at[0], halo_recv.at[0], {"ctx": blk - 1, "tp": me},
        )

    @pl.when(has_next)
    def _():
        fwd_halo().start()

    loads[2].wait()
    loads[3].wait()
    grad_gate(me)

    @pl.when(has_prev)
    def _():
        fwd_halo_in().wait_recv()

    @pl.when(jnp.logical_not(has_prev))
    def _():
        pext[:, 0:halo, :] = jnp.zeros((3, halo, channels), BF16)

    def lane(l):
        return pl.ds(pl.multiple_of(l * LANES, LANES), LANES)

    def correlate(lanes, count, base, sign):
        def tap_rows(q, acc):
            block = taps[pl.ds(pl.multiple_of(8 * q, 8), 8), lanes]
            start = pl.multiple_of(base + sign * 8 * q, 8)
            for r in range(8):
                acc = acc + block[r : r + 1] * shifted[r, pl.ds(start, count), :]
            return acc

        return lax.fori_loop(0, span // 8, tap_rows, jnp.zeros((count, LANES), F32))

    def forward(l, carry):
        lanes = lane(l)
        full = total + span
        streams = []
        for s in range(3):
            x = pext[s, :, lanes].astype(F32)
            st = short_ref[s, :, lanes]
            size = total if s == 0 else full
            low = halo + total - size
            acc = jnp.zeros((size, LANES), F32)
            for j in range(shorts):
                acc = acc + st[j : j + 1] * x[low - j : low - j + size]
            streams.append(acc.astype(BF16))
            if s == 0:
                query[:, lanes] = streams[0].astype(F32)
            else:
                bext[s, 0:total, lanes] = streams[s][span:]
        mixed = streams[1].astype(F32) * streams[2].astype(F32)
        for r in range(8):
            shifted[r, 8:full, :] = mixed[8 - r : full - r]
        half = total // 2
        for b in range(2):
            at = slice(b * half, (b + 1) * half)
            value = correlate(lanes, half, b * half + span, -1)
            inner[at, lanes] = value
            gated[at, lanes] = (query[at, lanes] * value).astype(BF16)
        return carry

    def grad_step(k):
        if k < n:
            step(grads, gg, k, grad_gate)

    lax.fori_loop(0, tiles // 2, forward, 0)
    grad_step(1)
    lax.fori_loop(tiles // 2, tiles, forward, 0)

    chunk = min(1024, width)

    def part_out(shard, d):
        at = pl.ds(pl.multiple_of(shard * rows, 16), rows)
        return jnp.dot(gated[at, :], o[:, d : d + chunk], preferred_element_type=F32)

    def part_act(shard, d):
        at = pl.ds(pl.multiple_of(shard * rows, 16), rows)
        value = None
        for s in range(3):
            term = lax.dot_general(
                gproj[s, at, :], w[s, d : d + chunk, :], NT, preferred_element_type=F32
            )
            value = term if value is None else value + term
        return value

    def fill(buf, part, shard):
        for d in range(0, width, chunk):
            buf[shard, :, d : d + chunk] = part(shard, d).astype(BF16)

    def add(buf, arrived, shard):
        for d in range(0, width, chunk):
            at = slice(d, d + chunk)
            buf[shard, :, at] = (
                buf[shard, :, at].astype(F32) + arrived[shard, :, at].astype(F32)
            ).astype(BF16)

    def r_copy(buf, land, s, shard, where):
        return to(buf.at[shard], land.at[shard], s[0].at[shard], s[1].at[shard], where)

    def l_copy(buf, land, s, shard, where):
        return to(buf.at[shard], land.at[shard], s[2].at[shard], s[3].at[shard], where)

    def reduce_step(t, buf, land_l, land_r, s, part):
        kr = t - me
        kl = t - (n - 1 - me)
        to_r, to_l = n - 1 - kr, kl
        go_r = (kr >= 0) & (to_r > me)
        go_l = (kl >= 0) & (to_l < me)

        @pl.when(go_r)
        def _():
            fill(buf, part, to_r)

            @pl.when(has_left)
            def _():
                r_copy(buf, land_l, s, to_r, left).wait_recv()
                add(buf, land_l, to_r)

            r_copy(buf, land_l, s, to_r, right).start()

        @pl.when(go_l)
        def _():
            fill(buf, part, to_l)

            @pl.when(has_right)
            def _():
                l_copy(buf, land_r, s, to_l, right).wait_recv()
                add(buf, land_r, to_l)

            l_copy(buf, land_r, s, to_l, left).start()

    def reduce_end(buf, land_l, land_r, s, part, result):
        for d in range(0, width, chunk):
            result[:, d : d + chunk] = part(me, d).astype(BF16)

        @pl.when(has_left)
        def _():
            r_copy(buf, land_l, s, me, left).wait_recv()

        @pl.when(has_right)
        def _():
            l_copy(buf, land_r, s, me, right).wait_recv()

        for cond, land in ((has_left, land_l), (has_right, land_r)):
            @pl.when(cond)
            def _(land=land):
                for d in range(0, width, chunk):
                    at = slice(d, d + chunk)
                    result[:, at] = (
                        result[:, at].astype(F32) + land[me, :, at].astype(F32)
                    ).astype(BF16)

        def one(i, carry):
            @pl.when(i > me)
            def _():
                r_copy(buf, land_l, s, i, right).wait_send()

            @pl.when(i < me)
            def _():
                l_copy(buf, land_r, s, i, left).wait_send()

            return carry

        lax.fori_loop(0, n, one, 0)

    out_args = (rs1, rs1_l, rs1_r, sems[8:12], part_out)
    act_args = (rs2, rs2_l, rs2_r, sems[12:16], part_act)

    grad_step(2)
    reduce_step(0, *out_args)
    for k in range(3, n):
        grad_step(k)

    def gate_back(l, carry):
        lanes = lane(l)
        g = ggate[:, lanes]
        gext[0:total, lanes] = (g * query[:, lanes]).astype(BF16)
        bext[0, 0:total, lanes] = (g * inner[:, lanes]).astype(BF16)
        return carry

    lax.fori_loop(0, tiles, gate_back, 0)

    def back_halo(where):
        return (
            to(gext.at[pl.ds(0, halo), :], gext.at[pl.ds(total, halo), :],
               halo_send.at[1], halo_recv.at[1], where),
            to(bext.at[:, pl.ds(0, 16), :], bext.at[:, pl.ds(total, 16), :],
               halo_send.at[2], halo_recv.at[2], where),
        )

    @pl.when(has_prev)
    def _():
        for copy in back_halo({"ctx": blk - 1, "tp": me}):
            copy.start()

    reduce_step(1, *out_args)

    @pl.when(has_next)
    def _():
        for copy in back_halo({"ctx": blk + 1, "tp": me}):
            copy.wait_recv()

    @pl.when(jnp.logical_not(has_next))
    def _():
        gext[total:, :] = jnp.zeros((halo, channels), BF16)
        bext[:, total:, :] = jnp.zeros((3, 16, channels), BF16)

    wide = total + 8

    def backward(l, carry):
        lanes = lane(l)
        x = gext[:, lanes].astype(F32)
        reach = total + halo - 8
        for r in range(8):
            shifted[r, 0:reach, :] = x[r : reach + r]
        count = wide // 3 if wide % 24 == 0 else wide
        mixed = jnp.concatenate(
            [correlate(lanes, count, b * count, 1) for b in range(wide // count)], axis=0
        )
        for s in range(3):
            other = bext[(0, 2, 1)[s], :, lanes].astype(F32)[0:wide]
            source = other if s == 0 else mixed * other
            st = short_ref[s, :, lanes]
            acc = jnp.zeros((total, LANES), F32)
            for j in range(shorts):
                acc = acc + st[j : j + 1] * source[j : j + total]
            gproj[s, :, lanes] = acc.astype(BF16)
        return carry

    lax.fori_loop(0, tiles // 2, backward, 0)
    for t in range(2, min(3, n - 1)):
        reduce_step(t, *out_args)
    lax.fori_loop(tiles // 2, tiles, backward, 0)
    for t in range(3, n - 1):
        reduce_step(t, *out_args)

    reduce_step(0, *act_args)
    reduce_end(*out_args, out_ref)
    for t in range(1, n - 1):
        reduce_step(t, *act_args)
    reduce_end(*act_args, dact_ref)

    gather_drain(acts, ga)
    gather_drain(grads, gg)

    @pl.when(has_next)
    def _():
        fwd_halo().wait_send()

    @pl.when(has_prev)
    def _():
        for copy in back_halo({"ctx": blk - 1, "tp": me}):
            copy.wait_send()


def body(activations, input_proj, short_taps, medium_taps, skip_gain, output_proj, out_grad):
    n = lax.axis_size("tp")
    blocks = lax.axis_size("ctx")
    rows, width = activations.shape
    channels = input_proj.shape[2]
    total = rows * n
    span = medium_taps.shape[1]
    lead = short_taps.shape[1] - 1
    halo = -(-(span + lead) // 16) * 16
    any_spec = pl.BlockSpec(memory_space=pl.ANY)
    vmem = pl.BlockSpec(memory_space=pltpu.VMEM)
    line = pltpu.VMEM((n, rows, width), BF16)
    dma = pltpu.SemaphoreType.DMA
    return pl.pallas_call(
        functools.partial(kernel, n, blocks, halo, lead),
        name="hyena",
        out_shape=(
            jax.ShapeDtypeStruct((rows, width), BF16),
            jax.ShapeDtypeStruct((rows, width), BF16),
        ),
        in_specs=[any_spec, any_spec, vmem, vmem, vmem, any_spec, any_spec],
        out_specs=(vmem, vmem),
        scratch_shapes=[
            pltpu.VMEM((3, width, channels), BF16),
            pltpu.VMEM((channels, width), BF16),
            line,
            line,
            pltpu.VMEM((span, channels), F32),
            pltpu.VMEM((3, halo + total, channels), BF16),
            pltpu.VMEM((3, total + 16, channels), BF16),
            pltpu.VMEM((total + halo, channels), BF16),
            pltpu.VMEM((total, channels), F32),
            pltpu.VMEM((total, channels), F32),
            pltpu.VMEM((total, channels), BF16),
            pltpu.VMEM((total, channels), F32),
            pltpu.VMEM((3, total, channels), BF16),
            pltpu.VMEM((8, total + halo, LANES), F32),
            line, line, line, line, line, line,
            dma((4,)),
            dma((1,)),
            dma((3,)),
            dma((3,)),
        ]
        + [dma((n,))] * 16,
        compiler_params=pltpu.CompilerParams(
            collective_id=0, has_side_effects=True, vmem_limit_bytes=60 * 1024 * 1024
        ),
    )(
        activations,
        jnp.transpose(input_proj, (1, 0, 2)),
        short_taps,
        medium_taps,
        skip_gain.reshape(1, channels),
        output_proj,
        out_grad,
    )


def solution(mesh):
    placed = (
        P(("ctx", "tp"), None),
        P(None, None, "tp"),
        P(None, None, "tp"),
        P("tp", None),
        P("tp"),
        P("tp", None),
        P(("ctx", "tp"), None),
    )
    return jax.shard_map(
        body,
        mesh=mesh,
        in_specs=placed,
        out_specs=(P(("ctx", "tp"), None), P(("ctx", "tp"), None)),
        check_vma=False,
    )
```

time: 245 us -> 152 us (0.62)
  Pallas kernels: 0 us -> 147 us
  local copies, waits for them, and re-layouts: 102 us -> 3.74 us
  waiting for transfers between devices: 69.9 us -> 0 us
  matrix products: 39.9 us -> 0 us
  other arithmetic: 14 us -> 0 us
  between operations: 14.2 us -> 0.64 us
  starting transfers between devices: 3.45 us -> 0 us
    pallas_call x0 -> x1, Pallas kernels: none -> 147 us  [body(): pl.pallas_call(functools.partial(kernel, n, blocks, halo, lead), name='hy...]
    reduce_scatter x2 -> x0, waiting for transfers between devices: 47 us -> none  [the longest x1 47 us: body(): lax.psum_scatter(lax.dot_general(part, flat_proj, contract, preferred_ele...]
    convert_element_type x14 -> x0, local copies, waits for them, and re-layouts: 42.4 us -> none  [short_sum(): source[offset:offset + length].astype(jnp.float32)]
    dot_general x6 -> x0, matrix products: 39.9 us -> none  [the longest x2 11.9 us: grouped_conv(): jnp.einsum('gtk,bkgc->btgc', band, window, precision=lax.Precision.HIGHEST)]
    unnamed x40 -> x2, local copies, waits for them, and re-layouts: 28.1 us -> 3.74 us
    another operation x4 -> x0, local copies, waits for them, and re-layouts: 19.5 us -> none  [banded(): tiled = jnp.tile(padded, (1, row_count))[:, :row_count * col_count]]
    all_gather x2 -> x0, waiting for transfers between devices: 15.6 us -> none  [the longest x1 15.6 us: body(): lax.all_gather(activations, 'tp', axis=0, tiled=True)]
    convert_element_type x4 -> x0, other arithmetic: 13.5 us -> none  [the longest x1 7.33 us: body(): short_sum(extended, short_taps, conv_rows, True).astype(jnp.bfloat16)]
  transfers between devices with their start and end apart: 6 -> 0, of which waited for: 3 -> 0; matrix products, arithmetic and copies ran while one was open for 61% -> 0% of each run, Pallas kernels for 0% -> 0%
where the time goes in v1:
time: 152 us; the launch traced here: 151 us
  Pallas kernels  147 us (97%)
  local copies, waits for them, and re-layouts  3.74 us (2%)
    pallas_call x1, Pallas kernels, body(): pl.pallas_call(functools.partial(kernel, n, blocks, halo, lead), name='hy...  147 us
    unnamed x2, local copies, waits for them, and re-layouts  3.74 us

profile of v1, /device:TPU:0, one launch (start us, length us, event | category | flops | bytes accessed | tf_op | source)
XLA Modules:
  0.0 151.3 jit_solution(17521228207317237417)
XLA Ops:
  0.6 147.0 %hyena.1 = (bf16[64,4096]{1,0:T(8,128)(2,1)}, bf16[64,4096]{1,0:T(8,128)(2,1)}) custom-call(bf16[64,4096]{1,0:T(8,128)(2,1)} %act_hbm.1, bf16[3,4096,512]{2,1,0:T(8,128)(2,1)} %bitcast.2, f32[3,7,512]{2,1,0:T(8,128)} %short_ref.1, f32[32,128]{1,0:T(8,128)} %med_ref.1, f32[1,512]{1,0:T(1,128)} %bitcast.3, bf16[512,4096]{1,0:T(8,128)(2,1)} %o_hbm.1, ...), custom_call_target="tpu_custom_call" | custom-call | tf_op jit(solution)/shard_map/hyena/pallas_call | solution.py:454
  147.6 1.9 %copy.11 = bf16[64,4096]{1,0:T(8,128)(2,1)} copy(bf16[64,4096]{1,0:T(8,128)(2,1)} %get-tuple-element.4) | data formatting | bytes 1048576
  149.5 1.9 %copy.12 = bf16[64,4096]{1,0:T(8,128)(2,1)} copy(bf16[64,4096]{1,0:T(8,128)(2,1)} %get-tuple-element.5) | data formatting | bytes 1048576

commit v2 on v1

--- a/solution.py
+++ b/solution.py
@@ -68,29 +68,31 @@
     ga = sems[0:4]
     gg = sems[4:8]
 
-    def send_right(buf, own, s, shard, first):
-        src = own if first else buf.at[shard]
-        to(src, buf.at[shard], s[0].at[shard], s[1].at[shard], right).start()
-
-    def send_left(buf, own, s, shard, first):
-        src = own if first else buf.at[shard]
-        to(src, buf.at[shard], s[2].at[shard], s[3].at[shard], left).start()
-
-    def from_left(buf, s, shard):
-        to(buf.at[shard], buf.at[shard], s[0].at[shard], s[1].at[shard], left).wait_recv()
-
-    def from_right(buf, s, shard):
-        to(buf.at[shard], buf.at[shard], s[2].at[shard], s[3].at[shard], right).wait_recv()
+    half = width // 2
+
+    def cols(h):
+        return pl.ds(pl.multiple_of(h * half, LANES), half)
+
+    def piece(buf, s, shard, h, base, where, own=None):
+        at = buf.at[shard, :, cols(h)]
+        src = at if own is None else own.at[:, cols(h)]
+        i = 2 * shard + h
+        return to(src, at, s[base].at[i], s[base + 1].at[i], where)
+
+    def send_own(buf, own, s, base, where):
+        for h in range(2):
+            piece(buf, s, me, h, base, where, own).start()
 
     def gather_drain(buf, s):
         def one(i, carry):
-            @pl.when(has_right & (i <= me))
-            def _():
-                to(buf.at[i], buf.at[i], s[0].at[i], s[1].at[i], right).wait_send()
-
-            @pl.when(has_left & (i >= me))
-            def _():
-                to(buf.at[i], buf.at[i], s[2].at[i], s[3].at[i], left).wait_send()
+            for h in range(2):
+                @pl.when(has_right & (i <= me))
+                def _(h=h):
+                    piece(buf, s, i, h, 0, right).wait_send()
+
+                @pl.when(has_left & (i >= me))
+                def _(h=h):
+                    piece(buf, s, i, h, 2, left).wait_send()
 
             return carry
 
@@ -99,19 +101,19 @@
     def grad_own(step):
         @pl.when(has_right & (me == step))
         def _():
-            send_right(grads, grad_hbm, gg, me, True)
+            send_own(grads, grad_hbm, gg, 0, right)
 
         @pl.when(has_left & (n - 1 - me == step))
         def _():
-            send_left(grads, grad_hbm, gg, me, True)
+            send_own(grads, grad_hbm, gg, 2, left)
 
     @pl.when(has_right)
     def _():
-        send_right(acts, act_hbm, ga, me, True)
+        send_own(acts, act_hbm, ga, 0, right)
 
     @pl.when(has_left)
     def _():
-        send_left(acts, act_hbm, ga, me, True)
+        send_own(acts, act_hbm, ga, 2, left)
 
     grad_own(0)
 
@@ -135,45 +137,48 @@
         at = pl.ds(pl.multiple_of(shard * rows, 16), rows)
         ggate[at, :] = lax.dot_general(grads[shard], o[...], NT, preferred_element_type=F32)
 
-    def step(buf, s, k, use):
+    def pass_on(buf, s, k, h):
         l, r = me - k, me + k
 
         @pl.when(l >= 0)
         def _():
-            from_left(buf, s, l)
+            piece(buf, s, l, h, 0, left).wait_recv()
 
             @pl.when(has_right)
             def _():
-                send_right(buf, None, s, l, False)
+                piece(buf, s, l, h, 0, right).start()
 
         @pl.when(r < n)
         def _():
-            from_right(buf, s, r)
+            piece(buf, s, r, h, 2, right).wait_recv()
 
             @pl.when(has_left)
             def _():
-                send_left(buf, None, s, r, False)
-
-        if use is project:
-            grad_own(k)
-
-        @pl.when(l >= 0)
-        def _():
-            use(l)
-
-        @pl.when(r < n)
-        def _():
-            use(r)
+                piece(buf, s, r, h, 2, left).start()
 
     loads[0].wait()
     loads[1].wait()
-    project(me)
-
-    def act_step(k, carry):
-        step(acts, ga, k, project)
+
+    def act_step(i, carry):
+        k, h = 1 + i // 2, i % 2
+
+        @pl.when(i < 2 * (n - 1))
+        def _():
+            pass_on(acts, ga, k, h)
+
+        @pl.when((h == 1) & (k < n))
+        def _():
+            grad_own(k)
+
+        shard = jnp.where(h == 0, me + k - 1, me - k)
+
+        @pl.when((shard >= 0) & (shard < n))
+        def _():
+            project(shard)
+
         return carry
 
-    lax.fori_loop(1, n, act_step, 0)
+    lax.fori_loop(0, 2 * n - 1, act_step, 0)
 
     def fwd_halo():
         return to(
@@ -215,6 +220,23 @@
             return acc
 
         return lax.fori_loop(0, span // 8, tap_rows, jnp.zeros((count, LANES), F32))
+
+    def grad_step(i, carry):
+        k, h = 1 + i // 2, i % 2
+
+        @pl.when(k < n)
+        def _():
+            pass_on(grads, gg, k, h)
+
+            @pl.when((h == 1) & (me - k >= 0))
+            def _():
+                grad_gate(me - k)
+
+            @pl.when((h == 1) & (me + k < n))
+            def _():
+                grad_gate(me + k)
+
+        return carry
 
     def forward(l, carry):
         lanes = lane(l)
@@ -236,23 +258,17 @@
         mixed = streams[1].astype(F32) * streams[2].astype(F32)
         for r in range(8):
             shifted[r, 8:full, :] = mixed[8 - r : full - r]
-        half = total // 2
+        count = total // 2
         for b in range(2):
-            at = slice(b * half, (b + 1) * half)
-            value = correlate(lanes, half, b * half + span, -1)
+            at = slice(b * count, (b + 1) * count)
+            value = correlate(lanes, count, b * count + span, -1)
             inner[at, lanes] = value
             gated[at, lanes] = (query[at, lanes] * value).astype(BF16)
-        return carry
-
-    def grad_step(k):
-        if k < n:
-            step(grads, gg, k, grad_gate)
-
-    lax.fori_loop(0, tiles // 2, forward, 0)
-    grad_step(1)
-    lax.fori_loop(tiles // 2, tiles, forward, 0)
-
-    chunk = min(1024, width)
+        return grad_step(l, carry)
+
+    lax.fori_loop(0, tiles, forward, 0)
+
+    chunk = min(1024, half)
 
     def part_out(shard, d):
         at = pl.ds(pl.multiple_of(shard * rows, 16), rows)
@@ -268,81 +284,65 @@
             value = term if value is None else value + term
         return value
 
-    def fill(buf, part, shard):
-        for d in range(0, width, chunk):
+    def sum_copy(buf, land, s, shard, h, base, where):
+        i = 2 * shard + h
+        return to(
+            buf.at[shard, :, cols(h)], land.at[shard, :, cols(h)],
+            s[base].at[i], s[base + 1].at[i], where,
+        )
+
+    def hand_on(buf, land, s, part, shard, h, base, source, has_source, target):
+        for d in range(h * half, (h + 1) * half, chunk):
             buf[shard, :, d : d + chunk] = part(shard, d).astype(BF16)
 
-    def add(buf, arrived, shard):
-        for d in range(0, width, chunk):
-            at = slice(d, d + chunk)
+        @pl.when(has_source)
+        def _():
+            sum_copy(buf, land, s, shard, h, base, source).wait_recv()
+            at = slice(h * half, (h + 1) * half)
             buf[shard, :, at] = (
-                buf[shard, :, at].astype(F32) + arrived[shard, :, at].astype(F32)
+                buf[shard, :, at].astype(F32) + land[shard, :, at].astype(F32)
             ).astype(BF16)
 
-    def r_copy(buf, land, s, shard, where):
-        return to(buf.at[shard], land.at[shard], s[0].at[shard], s[1].at[shard], where)
-
-    def l_copy(buf, land, s, shard, where):
-        return to(buf.at[shard], land.at[shard], s[2].at[shard], s[3].at[shard], where)
+        sum_copy(buf, land, s, shard, h, base, target).start()
 
     def reduce_step(t, buf, land_l, land_r, s, part):
         kr = t - me
         kl = t - (n - 1 - me)
         to_r, to_l = n - 1 - kr, kl
-        go_r = (kr >= 0) & (to_r > me)
-        go_l = (kl >= 0) & (to_l < me)
-
-        @pl.when(go_r)
-        def _():
-            fill(buf, part, to_r)
-
-            @pl.when(has_left)
-            def _():
-                r_copy(buf, land_l, s, to_r, left).wait_recv()
-                add(buf, land_l, to_r)
-
-            r_copy(buf, land_l, s, to_r, right).start()
-
-        @pl.when(go_l)
-        def _():
-            fill(buf, part, to_l)
-
-            @pl.when(has_right)
-            def _():
-                l_copy(buf, land_r, s, to_l, right).wait_recv()
-                add(buf, land_r, to_l)
-
-            l_copy(buf, land_r, s, to_l, left).start()
+        for h in range(2):
+            @pl.when((kr >= 0) & (to_r > me))
+            def _(h=h):
+                hand_on(buf, land_l, s, part, to_r, h, 0, left, has_left, right)
+
+            @pl.when((kl >= 0) & (to_l < me))
+            def _(h=h):
+                hand_on(buf, land_r, s, part, to_l, h, 2, right, has_right, left)
 
     def reduce_end(buf, land_l, land_r, s, part, result):
         for d in range(0, width, chunk):
             result[:, d : d + chunk] = part(me, d).astype(BF16)
 
-        @pl.when(has_left)
-        def _():
-            r_copy(buf, land_l, s, me, left).wait_recv()
-
-        @pl.when(has_right)
-        def _():
-            l_copy(buf, land_r, s, me, right).wait_recv()
-
-        for cond, land in ((has_left, land_l), (has_right, land_r)):
-            @pl.when(cond)
-            def _(land=land):
-                for d in range(0, width, chunk):
-                    at = slice(d, d + chunk)
+        for h in range(2):
+            for cond, land, base, source in (
+                (has_left, land_l, 0, left), (has_right, land_r, 2, right)
+            ):
+                @pl.when(cond)
+                def _(h=h, land=land, base=base, source=source):
+                    sum_copy(buf, land, s, me, h, base, source).wait_recv()
+                    at = slice(h * half, (h + 1) * half)
                     result[:, at] = (
                         result[:, at].astype(F32) + land[me, :, at].astype(F32)
                     ).astype(BF16)
 
         def one(i, carry):
-            @pl.when(i > me)
-            def _():
-                r_copy(buf, land_l, s, i, right).wait_send()
-
-            @pl.when(i < me)
-            def _():
-                l_copy(buf, land_r, s, i, left).wait_send()
+            for h in range(2):
+                @pl.when(i > me)
+                def _(h=h):
+                    sum_copy(buf, land_l, s, i, h, 0, right).wait_send()
+
+                @pl.when(i < me)
+                def _(h=h):
+                    sum_copy(buf, land_r, s, i, h, 2, left).wait_send()
 
             return carry
 
@@ -351,10 +351,8 @@
     out_args = (rs1, rs1_l, rs1_r, sems[8:12], part_out)
     act_args = (rs2, rs2_l, rs2_r, sems[12:16], part_act)
 
-    grad_step(2)
     reduce_step(0, *out_args)
-    for k in range(3, n):
-        grad_step(k)
+    lax.fori_loop(tiles, max(tiles, 2 * (n - 1)), grad_step, 0)
 
     def gate_back(l, carry):
         lanes = lane(l)
@@ -481,7 +479,7 @@
             dma((3,)),
             dma((3,)),
         ]
-        + [dma((n,))] * 16,
+        + [dma((2 * n,))] * 16,
         compiler_params=pltpu.CompilerParams(
             collective_id=0, has_side_effects=True, vmem_limit_bytes=60 * 1024 * 1024
         ),

time: 152 us -> 139 us (0.914)
  Pallas kernels: 147 us -> 134 us
    pallas_call x1, Pallas kernels: 147 us -> 134 us  [body(): pl.pallas_call(functools.partial(kernel, n, blocks, halo, lead), name='hy...]
where the time goes in v2:
time: 139 us
  Pallas kernels  134 us (96%)
  local copies, waits for them, and re-layouts  3.74 us (3%)
    pallas_call x1, Pallas kernels, body(): pl.pallas_call(functools.partial(kernel, n, blocks, halo, lead), name='hy...  134 us
    unnamed x2, local copies, waits for them, and re-layouts  3.74 us

profile of v2, /device:TPU:0, one launch (start us, length us, event | category | flops | bytes accessed | tf_op | source)
XLA Modules:
  0.0 138.8 jit_solution(16727748230476967310)
XLA Ops:
  0.6 134.4 %hyena.1 = (bf16[64,4096]{1,0:T(8,128)(2,1)}, bf16[64,4096]{1,0:T(8,128)(2,1)}) custom-call(bf16[64,4096]{1,0:T(8,128)(2,1)} %act_hbm.1, bf16[3,4096,512]{2,1,0:T(8,128)(2,1)} %bitcast.2, f32[3,7,512]{2,1,0:T(8,128)} %short_ref.1, f32[32,128]{1,0:T(8,128)} %med_ref.1, f32[1,512]{1,0:T(1,128)} %bitcast.3, bf16[512,4096]{1,0:T(8,128)(2,1)} %o_hbm.1, ...), custom_call_target="tpu_custom_call" | custom-call | tf_op jit(solution)/shard_map/hyena/pallas_call | solution.py:452
  135.0 1.9 %copy.11 = bf16[64,4096]{1,0:T(8,128)(2,1)} copy(bf16[64,4096]{1,0:T(8,128)(2,1)} %get-tuple-element.4) | data formatting | bytes 1048576
  136.9 1.9 %copy.12 = bf16[64,4096]{1,0:T(8,128)(2,1)} copy(bf16[64,4096]{1,0:T(8,128)(2,1)} %get-tuple-element.5) | data formatting | bytes 1048576

commit v3 on v2

--- a/solution.py
+++ b/solution.py
@@ -268,7 +268,9 @@
 
     lax.fori_loop(0, tiles, forward, 0)
 
-    chunk = min(1024, half)
+    cuts = 4
+    cut = width // cuts
+    chunk = min(1024, cut)
 
     def part_out(shard, d):
         at = pl.ds(pl.multiple_of(shard * rows, 16), rows)
@@ -285,20 +287,20 @@
         return value
 
     def sum_copy(buf, land, s, shard, h, base, where):
-        i = 2 * shard + h
+        i = cuts * shard + h
         return to(
-            buf.at[shard, :, cols(h)], land.at[shard, :, cols(h)],
+            buf.at[shard, :, pl.ds(h * cut, cut)], land.at[shard, :, pl.ds(h * cut, cut)],
             s[base].at[i], s[base + 1].at[i], where,
         )
 
     def hand_on(buf, land, s, part, shard, h, base, source, has_source, target):
-        for d in range(h * half, (h + 1) * half, chunk):
+        for d in range(h * cut, (h + 1) * cut, chunk):
             buf[shard, :, d : d + chunk] = part(shard, d).astype(BF16)
 
         @pl.when(has_source)
         def _():
             sum_copy(buf, land, s, shard, h, base, source).wait_recv()
-            at = slice(h * half, (h + 1) * half)
+            at = slice(h * cut, (h + 1) * cut)
             buf[shard, :, at] = (
                 buf[shard, :, at].astype(F32) + land[shard, :, at].astype(F32)
             ).astype(BF16)
@@ -309,7 +311,7 @@
         kr = t - me
         kl = t - (n - 1 - me)
         to_r, to_l = n - 1 - kr, kl
-        for h in range(2):
+        for h in range(cuts):
             @pl.when((kr >= 0) & (to_r > me))
             def _(h=h):
                 hand_on(buf, land_l, s, part, to_r, h, 0, left, has_left, right)
@@ -322,20 +324,20 @@
         for d in range(0, width, chunk):
             result[:, d : d + chunk] = part(me, d).astype(BF16)
 
-        for h in range(2):
+        for h in range(cuts):
             for cond, land, base, source in (
                 (has_left, land_l, 0, left), (has_right, land_r, 2, right)
             ):
                 @pl.when(cond)
                 def _(h=h, land=land, base=base, source=source):
                     sum_copy(buf, land, s, me, h, base, source).wait_recv()
-                    at = slice(h * half, (h + 1) * half)
+                    at = slice(h * cut, (h + 1) * cut)
                     result[:, at] = (
                         result[:, at].astype(F32) + land[me, :, at].astype(F32)
                     ).astype(BF16)
 
         def one(i, carry):
-            for h in range(2):
+            for h in range(cuts):
                 @pl.when(i > me)
                 def _(h=h):
                     sum_copy(buf, land_l, s, i, h, 0, right).wait_send()
@@ -479,7 +481,8 @@
             dma((3,)),
             dma((3,)),
         ]
-        + [dma((2 * n,))] * 16,
+        + [dma((2 * n,))] * 8
+        + [dma((4 * n,))] * 8,
         compiler_params=pltpu.CompilerParams(
             collective_id=0, has_side_effects=True, vmem_limit_bytes=60 * 1024 * 1024
         ),

time: 139 us -> 139 us (level)
  no operation moved by 1% of the time
where the time goes in v3:
time: 139 us
  Pallas kernels  135 us (97%)
  local copies, waits for them, and re-layouts  3.74 us (3%)
    pallas_call x1, Pallas kernels, body(): pl.pallas_call(functools.partial(kernel, n, blocks, halo, lead), name='hy...  135 us
    unnamed x2, local copies, waits for them, and re-layouts  3.74 us

profile of v3, /device:TPU:0, one launch (start us, length us, event | category | flops | bytes accessed | tf_op | source)
XLA Modules:
  0.0 139.2 jit_solution(8795030949439379941)
XLA Ops:
  0.6 134.9 %hyena.1 = (bf16[64,4096]{1,0:T(8,128)(2,1)}, bf16[64,4096]{1,0:T(8,128)(2,1)}) custom-call(bf16[64,4096]{1,0:T(8,128)(2,1)} %act_hbm.1, bf16[3,4096,512]{2,1,0:T(8,128)(2,1)} %bitcast.2, f32[3,7,512]{2,1,0:T(8,128)} %short_ref.1, f32[32,128]{1,0:T(8,128)} %med_ref.1, f32[1,512]{1,0:T(1,128)} %bitcast.3, bf16[512,4096]{1,0:T(8,128)(2,1)} %o_hbm.1, ...), custom_call_target="tpu_custom_call" | custom-call | tf_op jit(solution)/shard_map/hyena/pallas_call | solution.py:454
  135.5 1.9 %copy.11 = bf16[64,4096]{1,0:T(8,128)(2,1)} copy(bf16[64,4096]{1,0:T(8,128)(2,1)} %get-tuple-element.4) | data formatting | bytes 1048576
  137.4 1.9 %copy.12 = bf16[64,4096]{1,0:T(8,128)(2,1)} copy(bf16[64,4096]{1,0:T(8,128)(2,1)} %get-tuple-element.5) | data formatting | bytes 1048576
